TPU v7x, 128 devices: a whole 4x4x4 slice. The times are simulated.
128 devices in a mesh: tm: 16 (over x, y), tile: 8 (over z, core).
Axes of the slice: x: 4, y: 4, z: 4, core: 2. Of those that a mesh axis runs over, the one named last changes fastest.
Arguments:
- observed: float32 [9, 64, 8192], P(None, 'tile', 'tm'), may hold values from -6 to 6
- increments: float32 [9, 64, 8192], P(None, 'tile', 'tm'), may hold values from -0.15625 to 0.15625
- model: float32 [512, 256], P(('tm', 'tile')), may hold values from -6 to 6
- kernel: bfloat16 [256, 4, 9, 256, 256], P(('tm', 'tile')), may hold values from -0.1875 to 0.1875
- tile_index: int32 [256, 4], P(('tm', 'tile')), may hold values from 0 to 511, all different within a row
- station_of: int32 [64, 8192], P('tile', 'tm'), may hold values from 0 to 65535, as said below
- line_length: int32 [64], P('tile'), may hold values from 2048 to 8192, as said below
Outputs:
- grad_model: float32 [512, 256], P(('tm', 'tile'))
- grad_increments: float32 [9, 64, 8192], P(None, 'tile', 'tm')
Inputs may be any that keep to these rules, and one draw needn't show every extreme that they name: `station_of`: in the samples of one index pair of tile and tm (its block of lines and block of time), no station tile (value // 256) holds more than 32 samples, and one holds exactly 32. `line_length`: some line has all 8192 samples. `tile_index`: each row names 4 different cell tiles, and every cell tile is named by some row.
All inputs are finite; a program needn't handle non-finite values.
Results may differ from a plain program's by a relative error of at most 0.0031.
Values may be sent and summed in bfloat16 or wider, within the bound.
A program may use at most 128 MiB of HBM per device.

v0:
```python
import math
import jax
import jax.numpy as jnp
from jax import lax
from jax.sharding import PartitionSpec as P


def prefix(part, axis, combine, identity, reverse):
    count = lax.axis_size(axis)
    place = lax.axis_index(axis)
    ahead = count - 1 - place if reverse else place
    gathered = lax.all_gather(part, axis)
    state = jnp.zeros_like(part) + jnp.asarray(identity, part.dtype)

    def one(turn, state):
        source = count - 1 - turn if reverse else turn
        return combine(state, lax.dynamic_index_in_dim(gathered, source, 0, False))

    return lax.fori_loop(0, ahead, one, state)


def running_sum(values, backward):
    components, line_count, step_count = values.shape
    block_size = 128
    pieces = values.reshape(components, line_count, step_count // block_size, block_size)
    rows_index = lax.broadcasted_iota(jnp.int32, (block_size, block_size), 0)
    cols_index = lax.broadcasted_iota(jnp.int32, (block_size, block_size), 1)
    if backward:
        triangle = (rows_index >= cols_index).astype(jnp.float32)
    else:
        triangle = (rows_index <= cols_index).astype(jnp.float32)
    within = jnp.matmul(pieces, triangle, precision=lax.Precision.HIGHEST)
    if backward:
        block_total = within[..., 0]
        offsets = jnp.flip(jnp.cumsum(jnp.flip(block_total, 2), axis=2), 2) - block_total
    else:
        block_total = within[..., -1]
        offsets = jnp.cumsum(block_total, axis=2) - block_total
    return (within + offsets[..., None]).reshape(values.shape)


def shards(observed, increments, model, kernel, tile_index, station_of, line_length):
    components, line_count, step_count = observed.shape
    tiles_here = kernel.shape[0]
    tile_width = kernel.shape[-1]
    time_devices = lax.axis_size("tm")
    device_count = time_devices * lax.axis_size("tile")
    station_count = tiles_here * device_count
    row_count = line_count * step_count
    capacity = 2 * row_count // station_count
    total_steps = step_count * time_devices
    line_total = line_count * lax.axis_size("tile")
    station_gain = 1.0 / math.sqrt(line_total * total_steps / (station_count * tile_width))
    own_index = lax.axis_index("tm")
    partial_walk = running_sum(increments, False)
    walk_totals = partial_walk[:, :, -1]
    earlier = prefix(walk_totals, "tm", jnp.add, jnp.zeros_like(walk_totals), False)
    drift_walk = partial_walk + earlier[:, :, None]
    positions = own_index * step_count + jnp.arange(step_count, dtype=jnp.int32)
    inside = positions[None, :] < line_length[:, None]
    offset = drift_walk - observed
    flat_station = station_of.reshape(row_count)
    flat_inside = inside.reshape(row_count)
    flat_offset = offset.reshape(components, row_count)
    whole_model = lax.all_gather(model.astype(jnp.bfloat16), ("tm", "tile"), axis=0, tiled=True)
    chosen = whole_model[tile_index]
    predicted = jnp.einsum("skcij,skj->csi", kernel, chosen, preferred_element_type=jnp.float32)
    tile_of_row = flat_station // tile_width
    inner_station = jnp.where(flat_inside, flat_station % tile_width, tile_width)
    ordering = jnp.argsort(tile_of_row, stable=True)
    sorted_tiles = tile_of_row[ordering]
    starts = jnp.searchsorted(sorted_tiles, jnp.arange(station_count, dtype=jnp.int32))
    placed = jnp.arange(row_count, dtype=jnp.int32) - starts[sorted_tiles]
    slot_sorted = sorted_tiles * capacity + placed
    slot_of_row = jnp.zeros((row_count,), jnp.int32).at[ordering].set(slot_sorted)
    outgoing = (
        jnp.zeros((components, station_count * capacity), jnp.float32)
        .at[:, slot_of_row]
        .set(flat_offset)
    )
    labels = (
        jnp.full((station_count * capacity,), tile_width, jnp.int32)
        .at[slot_of_row]
        .set(inner_station)
    )
    arrived, arrived_labels = (
        lax.all_to_all(
            outgoing.reshape(components, station_count, capacity),
            ("tm", "tile"),
            split_axis=1,
            concat_axis=2,
            tiled=True,
        ),
        lax.all_to_all(
            labels.reshape(1, station_count, capacity),
            ("tm", "tile"),
            split_axis=1,
            concat_axis=2,
            tiled=True,
        ),
    )
    occupied = arrived_labels < tile_width
    station_ids = jnp.arange(tile_width, dtype=jnp.int32)
    matches = (arrived_labels[0][:, :, None] == station_ids).astype(jnp.float32)
    picked = jnp.einsum("csi,sri->csr", predicted, matches, precision=lax.Precision.HIGHEST)
    answer = jnp.where(occupied, picked + arrived, 0.0)
    station_sums = jnp.einsum("csr,sri->csi", answer, matches, precision=lax.Precision.HIGHEST)
    station_half = (station_sums * station_gain).astype(jnp.bfloat16)
    returned = lax.all_to_all(
        answer.astype(jnp.bfloat16), ("tm", "tile"), split_axis=2, concat_axis=1, tiled=True
    ).astype(answer.dtype)
    residual = returned.reshape(components, station_count * capacity)[:, slot_of_row]
    contributions = jnp.einsum(
        "skcij,csi->skj", kernel, station_half, preferred_element_type=jnp.float32
    )
    cell_total = model.shape[0] * device_count
    local_grad = (
        jnp.zeros((cell_total, tile_width), jnp.float32)
        .at[tile_index.reshape(-1)]
        .add(contributions.reshape(-1, tile_width))
    )
    grad_model = lax.psum_scatter(local_grad, ("tm", "tile"), scatter_dimension=0, tiled=True)
    residual_block = residual.reshape(components, line_count, step_count)
    partial_tail = running_sum(residual_block, True)
    tail_totals = partial_tail[:, :, 0]
    remaining = prefix(tail_totals, "tm", jnp.add, jnp.zeros_like(tail_totals), True)
    grad_increments = (partial_tail + remaining[:, :, None]) / math.sqrt(total_steps)
    return (grad_model, grad_increments)


def solution(mesh):
    in_specs = (
        P(None, "tile", "tm"),
        P(None, "tile", "tm"),
        P(("tm", "tile"), None),
        P(("tm", "tile"), None, None, None, None),
        P(("tm", "tile"), None),
        P("tile", "tm"),
        P("tile"),
    )
    out_specs = (P(("tm", "tile"), None), P(None, "tile", "tm"))
    return jax.shard_map(shards, mesh=mesh, in_specs=in_specs, out_specs=out_specs, check_vma=False)
```

profile of v0, /device:TPU:1, one launch (start us, length us, event | category | flops | bytes accessed | tf_op | source)
XLA Modules:
  0.0 415.5 jit_solution(10348112344737669025)
XLA Ops:
  7.2 0.8 compare_bitcast_fusion
  8.0 0.7 copy.127
  8.7 5.8 %sort.17 = (s32[4096]{0:T(1024)}, s32[4096]{0:T(1024)S(1)}) sort(s32[4096]{0:T(1024)S(1)} %get-tuple-element.237, s32[4096]{0:T(1024)S(1)} %iota.37), dimensions={0}, to_apply=%region_0.0 | sort | flops 49152 | bytes 65536 | tf_op jit(solution)/shard_map/jit(argsort)/sort | solution.py:70
  14.5 23.0 %gather_fusion.1 = s32[4096]{0:T(1024)S(1)} fusion(s32[4096]{0:T(1024)S(1)} %get-tuple-element.237, s32[4096]{0:T(1024)S(1)} %get-tuple-element.238), kind=kCustom, calls=%fused_computation.1 | custom fusion | bytes 49152 | tf_op jit(solution)/shard_map/gather | solution.py:71
  37.6 23.3 %while.48 = (s32[]{:T(128)}, u32[256]{0:T(256)S(1)}, u32[256]{0:T(256)S(1)}, s32[4096]{0:T(1024)S(1)}, s32[]{:T(128)}, /*index=5*/s32[]{:T(128)}, s32[]{}) while((s32[]{:T(128)}, u32[256]{0:T(256)S(1)}, u32[256]{0:T(256)S(1)}, s32[4096]{0:T(1024)S(1)}, s32[]{:T(128)}, /*index=5*/s32[]{:T(128)}, s32[]{}) %tuple.85), condition=%wide.region_2.3_spmd.clone, body=%wide.region_1.2_spmd.clone.sunk | while | flops 4356 | bytes 16484 | solution.py:72
  37.6 1.7 gather_fusion
  39.4 1.7 gather_fusion
  41.2 1.7 gather_fusion
  43.0 1.7 gather_fusion
  44.8 1.7 gather_fusion
  46.6 1.7 gather_fusion
  48.4 1.7 gather_fusion
  50.2 1.7 gather_fusion
  52.0 1.7 gather_fusion
  53.8 1.7 gather_fusion
  55.6 1.7 gather_fusion
  57.3 1.7 gather_fusion
  59.1 1.7 gather_fusion
  60.9 25.7 %gather_fusion.2 = s32[4096]{0:T(1024)S(1)} fusion(s32[256]{0:T(256)S(1)} %convert_element_type.26, s32[4096]{0:T(1024)S(1)} %broadcast_clamp_fusion.1), kind=kCustom, calls=%fused_computation.2 | custom fusion | bytes 49152 | tf_op jit(solution)/shard_map/gather | solution.py:73
  86.7 15.5 %scatter_custom_fusion = s32[4096]{0:T(1024)S(1)} fusion(s32[4096]{0:T(1024)S(1)} %get-tuple-element.239, s32[4096]{0:T(1024)S(1)} %subtract_add_fusion, s32[]{:T(128)} %constant.112.clone.1), kind=kCustom, calls=%fused_computation.77 | custom fusion | bytes 16388 | tf_op jit(solution)/shard_map/scatter | solution.py:75
  102.3 15.5 %scatter_custom_fusion.1 = s32[8192]{0:T(1024)S(1)} fusion(s32[4096]{0:T(1024)S(1)} %get-tuple-element.235, s32[4096]{0:T(1024)S(1)} %get-tuple-element.236, s32[]{:T(128)} %constant.114.clone.1), kind=kCustom, calls=%fused_computation.67 | custom fusion | bytes 32772 | tf_op jit(solution)/shard_map/scatter | solution.py:84
  117.8 0.7 reshape.102
  118.6 11.5 %all-to-all-start = ((s32[1,256,32]{2,0,1:T(1,128)}), s32[1,256,32]{2,0,1:T(1,128)S(1)}, u32[]{:S(2)}, u32[]{:S(2)}) async-start(s32[1,256,32]{2,0,1:T(1,128)} %bitcast.5), calls=%async_computation | async-start | bytes 262144 | tf_op jit(solution)/shard_map/all_to_all | solution.py:94
  130.2 0.3 convolution_bitcast_fusion
  130.5 0.7 reduce-window_subtract_fusion
  131.2 0.3 copy.91
  131.5 0.1 broadcast_add_fusion.1
  132.0 18.4 %all-gather = f32[144,8,1]{1,2,0:T(1,128)S(1)} all-gather(f32[9,8,1]{1,2,0:T(1,128)S(1)} %copy.94), channel_id=2, replica_groups=mesh['tm'=16,'tile'=8] {'tm'}, dimensions={0}, use_global_device_ids=true | all-gather | bytes 4896 | tf_op jit(solution)/shard_map/all_gather | solution.py:12
  150.6 42.2 %all-gather.2 = bf16[128,4,256]{2,1,0:T(4,128)(2,1)S(1)} all-gather(bf16[1,4,256]{2,1,0:T(4,128)(2,1)S(1)} %convert_bitcast_fusion), channel_id=1, replica_groups=mesh['tm'=16,'tile'=8] {'tm','tile'}, dimensions={0}, use_global_device_ids=true | all-gather | bytes 264192 | tf_op jit(solution)/shard_map/all_gather | solution.py:65
  193.0 0.6 gather_fusion.3
  193.7 6.2 %convolution_bitcast_fusion.1 = f32[2,1,9,256,1]{3,1,4,2,0:T(1,128)S(1)} fusion(bf16[2,4,9,256,256]{4,3,2,1,0:T(8,128)(2,1)} %param.16, bf16[2,4,256,1,1]{2,3,1,4,0:T(2,128)(2,1)S(1)} %reshape.204), kind=kOutput, calls=%fused_computation.30 | convolution fusion | flops 9437184 | bytes 9459712 | tf_op jit(solution)/shard_map/skcij,skj->csi/dot_general | solution.py:67
  199.9 0.7 copy.122
  200.6 12.8 %scatter_custom_fusion.2 = f32[9,8192]{0,1:T(8,128)} fusion(s32[4096]{0:T(1024)S(1)} %get-tuple-element.235, f32[4096,9]{1,0:T(8,128)S(1)} %bitcast.115, f32[]{:T(128)} %constant.111.clone.1), kind=kCustom, calls=%fused_computation.24 | custom fusion | bytes 294916 | tf_op jit(solution)/shard_map/scatter | solution.py:79
  213.3 3.3 copy.99
  216.6 1.4 reshape.213
  218.1 4.7 %all-to-all-start.1 = ((f32[128,1,576]{2,1,0:T(1,128)}), f32[128,1,576]{2,1,0:T(1,128)S(1)}, u32[]{:S(2)}, u32[]{:S(2)}) async-start(f32[128,1,576]{2,1,0:T(1,128)} %reshape.213), calls=%async_computation.1 | async-start | bytes 655360 | tf_op jit(solution)/shard_map/all_to_all | solution.py:87
  222.9 3.9 fusion.5
  226.8 7.5 %all-to-all-done.1 = f32[128,1,576]{2,1,0:T(1,128)S(1)} async-done(((f32[128,1,576]{2,1,0:T(1,128)}), f32[128,1,576]{2,1,0:T(1,128)S(1)}, u32[]{:S(2)}, u32[]{:S(2)}) %all-to-all-start.1) | async-done | bytes 294944 | tf_op jit(solution)/shard_map/all_to_all | solution.py:87
  234.3 0.5 broadcast.166
  234.8 1.4 reduce
  236.2 0.6 reshape.214
  236.8 0.4 copy.100
  237.2 0.1 copy.101
  237.3 0.6 all_to_all.41
  238.0 0.4 fusion.37
  238.3 2.8 copy.103
  241.2 4.8 %reshape.215 = bf16[128,2,288]{2,1,0:T(2,128)(2,1)} reshape(bf16[4096,2,9]{2,1,0:T(2,128)(2,1)S(1)} %bitcast.110) | data formatting | bytes 294912
  246.0 4.7 %all-to-all-start.2 = ((bf16[128,2,288]{2,1,0:T(2,128)(2,1)}), bf16[128,2,288]{2,1,0:T(2,128)(2,1)S(1)}, u32[]{:S(2)}, u32[]{:S(2)}) async-start(bf16[128,2,288]{2,1,0:T(2,128)(2,1)} %reshape.215), calls=%async_computation.2 | async-start | bytes 393216 | tf_op jit(solution)/shard_map/all_to_all | solution.py:109
  250.6 0.3 all-reduce.3.cloned.1.call-start
  250.9 3.0 fusion.12
  253.9 5.0 %fusion.26 = f32[2,1,4,256,1]{3,1,4,2,0:T(1,128)S(1)} fusion(bf16[2,4,9,256,256]{4,3,2,1,0:T(8,128)(2,1)} %param.16, bf16[9,2,256,1,1]{2,0,1,3,4:T(8,128)(2,1)S(1)} %fusion.12), kind=kOutput, calls=%fused_computation.60 | convolution fusion | flops 9437184 | bytes 9454592 | tf_op jit(solution)/shard_map/skcij,csi->skj/dot_general | solution.py:113
  258.9 1.4 scatter_custom_fusion.3
  260.4 0.6 all-to-all-done.2
  260.9 4.9 %reshape.216 = bf16[4096,2,9]{2,1,0:T(2,128)(2,1)S(1)} reshape(bf16[128,2,288]{2,1,0:T(2,128)(2,1)S(1)} %all-to-all-done.2) | data formatting | bytes 294912
  265.8 1.9 copy.124
  267.7 12.9 %gather_fusion.4 = bf16[4096,9]{1,0:T(8,128)(2,1)S(1)} fusion(bf16[9,8192]{0,1:T(8,128)(2,1)} %bitcast.113, s32[4096]{0:T(1024)S(1)} %get-tuple-element.234), kind=kCustom, calls=%fused_computation.4 | custom fusion | bytes 163840 | tf_op jit(solution)/shard_map/gather | solution.py:112
  280.6 0.4 fusion.22
  281.1 0.3 copy.107
  281.5 0.1 broadcast_add_fusion
  281.9 18.6 %all-gather.1 = f32[144,8,1]{1,2,0:T(1,128)S(1)} all-gather(f32[9,8,1]{1,2,0:T(1,128)S(1)} %copy.110), channel_id=3, replica_groups=mesh['tm'=16,'tile'=8] {'tm'}, dimensions={0}, use_global_device_ids=true | all-gather | bytes 4896 | tf_op jit(solution)/shard_map/all_gather | solution.py:12
  300.7 0.8 while.47
  301.6 0.8 add_multiply_fusion
  302.4 105.0 %all-reduce.3.cloned.1.call-done = f32[512,256]{1,0:T(8,128)} async-done(((f32[512,256]{1,0:T(8,128)}), f32[512,256]{1,0:T(8,128)}) %all-reduce.3.cloned.1.call-update) | async-done | bytes 524304
  407.4 1.3 constant_dynamic-slice_fusion.2
  (125 shorter events, 2.4 us)
Async XLA Ops:
  7.2 123.0 %copy-start = (f32[9,8,512]{2,1,0:T(8,128)S(1)}, f32[9,8,512]{2,1,0:T(8,128)}, u32[]{:S(2)}) copy-start(f32[9,8,512]{2,1,0:T(8,128)} %param.14) | copy-start | bytes 442372
  60.9 69.2 %copy-start.3 = (s32[2,4]{1,0:T(2,128)S(1)}, s32[2,4]{1,0:T(2,128)}, u32[]{:S(2)}) copy-start(s32[2,4]{1,0:T(2,128)} %param.17) | copy-start | bytes 100
  60.9 89.7 %copy-start.2 = (f32[4,256]{1,0:T(4,128)S(1)}, f32[4,256]{1,0:T(4,128)}, u32[]{:S(2)}) copy-start(f32[4,256]{1,0:T(4,128)} %param.15) | copy-start | bytes 12292
  86.7 106.9 %copy-start.1 = (f32[9,8,512]{2,1,0:T(8,128)S(1)}, f32[9,8,512]{2,1,0:T(8,128)}, u32[]{:S(2)}) copy-start(f32[9,8,512]{2,1,0:T(8,128)} %param.13) | copy-start | bytes 442372
  118.6 99.5 %all-to-all-start = ((s32[1,256,32]{2,0,1:T(1,128)}), s32[1,256,32]{2,0,1:T(1,128)S(1)}, u32[]{:S(2)}, u32[]{:S(2)}) async-start(s32[1,256,32]{2,0,1:T(1,128)} %bitcast.5), calls=%async_computation | async-start | bytes 262144 | tf_op jit(solution)/shard_map/all_to_all | solution.py:94
  218.1 16.2 %all-to-all-start.1 = ((f32[128,1,576]{2,1,0:T(1,128)}), f32[128,1,576]{2,1,0:T(1,128)S(1)}, u32[]{:S(2)}, u32[]{:S(2)}) async-start(f32[128,1,576]{2,1,0:T(1,128)} %reshape.213), calls=%async_computation.1 | async-start | bytes 655360 | tf_op jit(solution)/shard_map/all_to_all | solution.py:87
  246.0 15.0 %all-to-all-start.2 = ((bf16[128,2,288]{2,1,0:T(2,128)(2,1)}), bf16[128,2,288]{2,1,0:T(2,128)(2,1)S(1)}, u32[]{:S(2)}, u32[]{:S(2)}) async-start(bf16[128,2,288]{2,1,0:T(2,128)(2,1)} %reshape.215), calls=%async_computation.2 | async-start | bytes 393216 | tf_op jit(solution)/shard_map/all_to_all | solution.py:109
  250.6 156.8 %all-reduce.3.cloned.1.call-start = ((), (), s32[]{:S(2)}) async-start(), calls=%async_computation.3 | async-start | bytes 1048576
Sparse Core Ops, SparseCore 0:
  260.5 146.8 all-reduce.2
where the time goes:
time: 416 us
  local copies, waits for them, and re-layouts  155 us (37%)
  waiting for transfers between devices  113 us (27%)
  blocking collectives  79.2 us (19%)
  starting transfers between devices  21.1 us (5%)
  matrix products  18.8 us (5%)
  between operations  14.5 us (3%)
  other arithmetic  12.3 us (3%)
    unnamed x2, waiting for transfers between devices  105 us
    all_gather x1, blocking collectives, shards(): lax.all_gather(model.astype(jnp.bfloat16), ('tm', 'tile'), axis=0, tiled=...  42.2 us
    all_gather x2, blocking collectives, prefix(): gathered = lax.all_gather(part, axis)  37 us
    gather x1, local copies, waits for them, and re-layouts, shards(): placed = jnp.arange(row_count, dtype=jnp.int32) - starts[sorted_tiles]  25.7 us
    gather x1, local copies, waits for them, and re-layouts, shards(): sorted_tiles = tile_of_row[ordering]  23 us
    gather x13, local copies, waits for them, and re-layouts, shards(): jnp.searchsorted(sorted_tiles, jnp.arange(station_count, dtype=jnp.int32))  22.4 us
    scatter x1, local copies, waits for them, and re-layouts, shards(): labels = jnp.full((station_count * capacity,), tile_width, jnp.int32).at[...  15.5 us
    scatter x1, local copies, waits for them, and re-layouts, shards(): jnp.zeros((row_count,), jnp.int32).at[ordering].set(slot_sorted)  15.5 us
  transfers between devices with their start and end apart: 4, of which 3 were waited for; matrix products, arithmetic and copies ran while one was open for 15% of the time, Pallas kernels for 0%

commit v1 on v0

--- a/solution.py
+++ b/solution.py
@@ -62,7 +62,15 @@
     flat_station = station_of.reshape(row_count)
     flat_inside = inside.reshape(row_count)
     flat_offset = offset.reshape(components, row_count)
-    whole_model = lax.all_gather(model.astype(jnp.bfloat16), ("tm", "tile"), axis=0, tiled=True)
+    whole_model = jnp.concatenate(
+        lax.all_to_all(
+            jnp.stack([model.astype(jnp.bfloat16)] * lax.axis_size(("tm", "tile"))),
+            ("tm", "tile"),
+            0,
+            0,
+        ),
+        axis=0,
+    )
     chosen = whole_model[tile_index]
     predicted = jnp.einsum("skcij,skj->csi", kernel, chosen, preferred_element_type=jnp.float32)
     tile_of_row = flat_station // tile_width

time: 416 us -> 396 us (0.952)
  blocking collectives: 79.2 us -> 36.8 us
  starting transfers between devices: 21.1 us -> 38.9 us
    all_gather x1 -> x0, blocking collectives: 42.2 us -> none  [shards(): lax.all_gather(model.astype(jnp.bfloat16), ('tm', 'tile'), axis=0, tiled=...]
    all_to_all x0 -> x1, starting transfers between devices: none -> 13.7 us  [shards(): lax.all_to_all(jnp.stack([model.astype(jnp.bfloat16)] * lax.axis_size(('t...]
    all_to_all x0 -> x1, waiting for transfers between devices: none -> 10.8 us  [shards(): lax.all_to_all(jnp.stack([model.astype(jnp.bfloat16)] * lax.axis_size(('t...]
    all_to_all x1, waiting for transfers between devices: 7.51 us -> 0.96 us  [shards(): lax.all_to_all(outgoing.reshape(components, station_count, capacity), ('t...]
    all_to_all x1, starting transfers between devices: 4.65 us -> 8.96 us  [shards(): lax.all_to_all(answer.astype(jnp.bfloat16), ('tm', 'tile'), split_axis=2,...]
    unnamed x16 -> x15, local copies, waits for them, and re-layouts: 13.8 us -> 13.7 us
  transfers between devices with their start and end apart: 4 -> 5, of which waited for: 3 -> 4; matrix products, arithmetic and copies ran while one was open for 15% -> 16% of each run, Pallas kernels for 0% -> 0%
where the time goes in v1:
time: 396 us
  local copies, waits for them, and re-layouts  156 us (39%)
  waiting for transfers between devices  117 us (30%)
  starting transfers between devices  38.9 us (10%)
  blocking collectives  36.8 us (9%)
  matrix products  18.8 us (5%)
  between operations  14.5 us (4%)
  other arithmetic  12.3 us (3%)
    unnamed x2, waiting for transfers between devices  105 us
    all_gather x2, blocking collectives, prefix(): gathered = lax.all_gather(part, axis)  36.8 us
    gather x1, local copies, waits for them, and re-layouts, shards(): placed = jnp.arange(row_count, dtype=jnp.int32) - starts[sorted_tiles]  25.7 us
    gather x1, local copies, waits for them, and re-layouts, shards(): sorted_tiles = tile_of_row[ordering]  23 us
    gather x13, local copies, waits for them, and re-layouts, shards(): jnp.searchsorted(sorted_tiles, jnp.arange(station_count, dtype=jnp.int32))  22.4 us
    scatter x1, local copies, waits for them, and re-layouts, shards(): labels = jnp.full((station_count * capacity,), tile_width, jnp.int32).at[...  15.5 us
    scatter x1, local copies, waits for them, and re-layouts, shards(): jnp.zeros((row_count,), jnp.int32).at[ordering].set(slot_sorted)  15.5 us
    all_to_all x1, starting transfers between devices, shards(): lax.all_to_all(jnp.stack([model.astype(jnp.bfloat16)] * lax.axis_size(('t...  13.7 us
  transfers between devices with their start and end apart: 5, of which 4 were waited for; matrix products, arithmetic and copies ran while one was open for 16% of the time, Pallas kernels for 0%

profile of v1, /device:TPU:1, one launch (start us, length us, event | category | flops | bytes accessed | tf_op | source)
XLA Modules:
  0.0 396.0 jit_solution(16673762703003015741)
XLA Ops:
  7.2 0.8 compare_bitcast_fusion
  8.0 0.7 copy.127
  8.7 5.8 %sort.17 = (s32[4096]{0:T(1024)}, s32[4096]{0:T(1024)S(1)}) sort(s32[4096]{0:T(1024)S(1)} %get-tuple-element.237, s32[4096]{0:T(1024)S(1)} %iota.37), dimensions={0}, to_apply=%region_0.0 | sort | flops 49152 | bytes 65536 | tf_op jit(solution)/shard_map/jit(argsort)/sort | solution.py:78
  14.5 23.0 %gather_fusion.1 = s32[4096]{0:T(1024)S(1)} fusion(s32[4096]{0:T(1024)S(1)} %get-tuple-element.237, s32[4096]{0:T(1024)S(1)} %get-tuple-element.238), kind=kCustom, calls=%fused_computation.1 | custom fusion | bytes 49152 | tf_op jit(solution)/shard_map/gather | solution.py:79
  37.6 23.3 %while.48 = (s32[]{:T(128)}, u32[256]{0:T(256)S(1)}, u32[256]{0:T(256)S(1)}, s32[4096]{0:T(1024)S(1)}, s32[]{:T(128)}, /*index=5*/s32[]{:T(128)}, s32[]{}) while((s32[]{:T(128)}, u32[256]{0:T(256)S(1)}, u32[256]{0:T(256)S(1)}, s32[4096]{0:T(1024)S(1)}, s32[]{:T(128)}, /*index=5*/s32[]{:T(128)}, s32[]{}) %tuple.85), condition=%wide.region_2.3_spmd.clone, body=%wide.region_1.2_spmd.clone.sunk | while | flops 4356 | bytes 16484 | solution.py:80
  37.6 1.7 gather_fusion
  39.4 1.7 gather_fusion
  41.2 1.7 gather_fusion
  43.0 1.7 gather_fusion
  44.8 1.7 gather_fusion
  46.6 1.7 gather_fusion
  48.4 1.7 gather_fusion
  50.2 1.7 gather_fusion
  52.0 1.7 gather_fusion
  53.8 1.7 gather_fusion
  55.6 1.7 gather_fusion
  57.3 1.7 gather_fusion
  59.1 1.7 gather_fusion
  60.9 25.7 %gather_fusion.2 = s32[4096]{0:T(1024)S(1)} fusion(s32[256]{0:T(256)S(1)} %convert_element_type.26, s32[4096]{0:T(1024)S(1)} %broadcast_clamp_fusion.1), kind=kCustom, calls=%fused_computation.2 | custom fusion | bytes 49152 | tf_op jit(solution)/shard_map/gather | solution.py:81
  86.7 15.5 %scatter_custom_fusion = s32[4096]{0:T(1024)S(1)} fusion(s32[4096]{0:T(1024)S(1)} %get-tuple-element.239, s32[4096]{0:T(1024)S(1)} %subtract_add_fusion, s32[]{:T(128)} %constant.112.clone.1), kind=kCustom, calls=%fused_computation.77 | custom fusion | bytes 16388 | tf_op jit(solution)/shard_map/scatter | solution.py:83
  102.2 15.5 %scatter_custom_fusion.1 = s32[8192]{0:T(1024)S(1)} fusion(s32[4096]{0:T(1024)S(1)} %get-tuple-element.235, s32[4096]{0:T(1024)S(1)} %get-tuple-element.236, s32[]{:T(128)} %constant.114.clone.1), kind=kCustom, calls=%fused_computation.67 | custom fusion | bytes 32772 | tf_op jit(solution)/shard_map/scatter | solution.py:92
  117.8 0.7 reshape.107
  118.6 11.5 %all-to-all-start = ((s32[1,256,32]{2,0,1:T(1,128)}), s32[1,256,32]{2,0,1:T(1,128)S(1)}, u32[]{:S(2)}, u32[]{:S(2)}) async-start(s32[1,256,32]{2,0,1:T(1,128)} %bitcast.5), calls=%async_computation | async-start | bytes 262144 | tf_op jit(solution)/shard_map/all_to_all | solution.py:102
  130.2 0.3 convolution_bitcast_fusion
  130.5 0.7 reduce-window_subtract_fusion
  131.2 0.3 copy.91
  131.5 0.1 broadcast_add_fusion.1
  132.0 18.4 %all-gather = f32[144,8,1]{1,2,0:T(1,128)S(1)} all-gather(f32[9,8,1]{1,2,0:T(1,128)S(1)} %copy.94), channel_id=2, replica_groups=mesh['tm'=16,'tile'=8] {'tm'}, dimensions={0}, use_global_device_ids=true | all-gather | bytes 4896 | tf_op jit(solution)/shard_map/all_gather | solution.py:12
  150.8 0.6 copy.122
  151.5 12.8 %scatter_custom_fusion.2 = f32[9,8192]{0,1:T(8,128)} fusion(s32[4096]{0:T(1024)S(1)} %get-tuple-element.235, f32[4096,9]{1,0:T(8,128)S(1)} %bitcast.113, f32[]{:T(128)} %constant.111.clone.1), kind=kCustom, calls=%fused_computation.24 | custom fusion | bytes 294916 | tf_op jit(solution)/shard_map/scatter | solution.py:87
  164.2 3.3 copy.99
  167.5 1.4 reshape.217
  169.0 0.8 stack.2
  169.7 13.7 %all-to-all-start.1 = ((bf16[128,4,256]{2,1,0:T(4,128)(2,1)}), bf16[128,4,256]{2,1,0:T(4,128)(2,1)S(1)}, u32[]{:S(2)}, u32[]{:S(2)}) async-start(bf16[128,4,256]{2,1,0:T(4,128)(2,1)} %stack.2), calls=%async_computation.1 | async-start | bytes 524288 | tf_op jit(solution)/shard_map/all_to_all | solution.py:66
  183.6 10.8 %all-to-all-done.1 = bf16[128,4,256]{2,1,0:T(4,128)(2,1)S(1)} async-done(((bf16[128,4,256]{2,1,0:T(4,128)(2,1)}), bf16[128,4,256]{2,1,0:T(4,128)(2,1)S(1)}, u32[]{:S(2)}, u32[]{:S(2)}) %all-to-all-start.1) | async-done | bytes 262176 | tf_op jit(solution)/shard_map/all_to_all | solution.py:66
  194.4 4.7 %all-to-all-start.2 = ((f32[128,1,576]{2,1,0:T(1,128)}), f32[128,1,576]{2,1,0:T(1,128)S(1)}, u32[]{:S(2)}, u32[]{:S(2)}) async-start(f32[128,1,576]{2,1,0:T(1,128)} %reshape.217), calls=%async_computation.2 | async-start | bytes 655360 | tf_op jit(solution)/shard_map/all_to_all | solution.py:95
  199.1 0.6 gather_fusion.3
  199.7 6.2 %convolution_bitcast_fusion.1 = f32[2,1,9,256,1]{3,1,4,2,0:T(1,128)S(1)} fusion(bf16[2,4,9,256,256]{4,3,2,1,0:T(8,128)(2,1)} %param.16, bf16[2,4,256,1,1]{2,3,1,4,0:T(2,128)(2,1)S(1)} %reshape.208), kind=kOutput, calls=%fused_computation.30 | convolution fusion | flops 9437184 | bytes 9459712 | tf_op jit(solution)/shard_map/skcij,skj->csi/dot_general | solution.py:75
  205.9 3.9 fusion.5
  209.8 1.0 all-to-all-done.2
  210.8 0.5 broadcast.168
  211.3 1.4 reduce
  212.7 0.6 reshape.218
  213.3 0.4 copy.100
  213.8 0.6 all_to_all.45
  214.4 0.4 fusion.37
  214.8 2.8 copy.103
  217.6 4.7 %reshape.219 = bf16[128,2,288]{2,1,0:T(2,128)(2,1)} reshape(bf16[4096,2,9]{2,1,0:T(2,128)(2,1)S(1)} %bitcast.108) | data formatting | bytes 294912
  222.4 9.0 %all-to-all-start.3 = ((bf16[128,2,288]{2,1,0:T(2,128)(2,1)}), bf16[128,2,288]{2,1,0:T(2,128)(2,1)S(1)}, u32[]{:S(2)}, u32[]{:S(2)}) async-start(bf16[128,2,288]{2,1,0:T(2,128)(2,1)} %reshape.219), calls=%async_computation.3 | async-start | bytes 393216 | tf_op jit(solution)/shard_map/all_to_all | solution.py:117
  231.4 3.0 fusion.12
  234.4 5.0 %fusion.26 = f32[2,1,4,256,1]{3,1,4,2,0:T(1,128)S(1)} fusion(bf16[2,4,9,256,256]{4,3,2,1,0:T(8,128)(2,1)} %param.16, bf16[9,2,256,1,1]{2,0,1,3,4:T(8,128)(2,1)S(1)} %fusion.12), kind=kOutput, calls=%fused_computation.60 | convolution fusion | flops 9437184 | bytes 9454592 | tf_op jit(solution)/shard_map/skcij,csi->skj/dot_general | solution.py:121
  239.4 1.4 scatter_custom_fusion.3
  240.9 0.7 all-to-all-done.3
  241.6 4.9 %reshape.220 = bf16[4096,2,9]{2,1,0:T(2,128)(2,1)S(1)} reshape(bf16[128,2,288]{2,1,0:T(2,128)(2,1)S(1)} %all-to-all-done.3) | data formatting | bytes 294912
  246.5 1.9 copy.124
  248.4 12.9 %gather_fusion.4 = bf16[4096,9]{1,0:T(8,128)(2,1)S(1)} fusion(bf16[9,8192]{0,1:T(8,128)(2,1)} %bitcast.111, s32[4096]{0:T(1024)S(1)} %get-tuple-element.234), kind=kCustom, calls=%fused_computation.4 | custom fusion | bytes 163840 | tf_op jit(solution)/shard_map/gather | solution.py:120
  261.3 0.4 fusion.22
  261.7 0.3 copy.107
  262.2 0.1 broadcast_add_fusion
  262.5 18.4 %all-gather.1 = f32[144,8,1]{1,2,0:T(1,128)S(1)} all-gather(f32[9,8,1]{1,2,0:T(1,128)S(1)} %copy.110), channel_id=3, replica_groups=mesh['tm'=16,'tile'=8] {'tm'}, dimensions={0}, use_global_device_ids=true | all-gather | bytes 4896 | tf_op jit(solution)/shard_map/all_gather | solution.py:12
  281.1 0.8 while.47
  282.0 0.8 add_multiply_fusion
  282.8 105.0 %all-reduce.3.cloned.1.call-done = f32[512,256]{1,0:T(8,128)} async-done(((f32[512,256]{1,0:T(8,128)}), f32[512,256]{1,0:T(8,128)}) %all-reduce.3.cloned.1.call-update) | async-done | bytes 524304
  387.8 1.3 constant_dynamic-slice_fusion.2
  (127 shorter events, 2.6 us)
Async XLA Ops:
  7.2 123.0 %copy-start = (f32[9,8,512]{2,1,0:T(8,128)S(1)}, f32[9,8,512]{2,1,0:T(8,128)}, u32[]{:S(2)}) copy-start(f32[9,8,512]{2,1,0:T(8,128)} %param.14) | copy-start | bytes 442372
  60.9 69.2 %copy-start.3 = (s32[2,4]{1,0:T(2,128)S(1)}, s32[2,4]{1,0:T(2,128)}, u32[]{:S(2)}) copy-start(s32[2,4]{1,0:T(2,128)} %param.17) | copy-start | bytes 100
  60.9 89.8 %copy-start.1 = (f32[9,8,512]{2,1,0:T(8,128)S(1)}, f32[9,8,512]{2,1,0:T(8,128)}, u32[]{:S(2)}) copy-start(f32[9,8,512]{2,1,0:T(8,128)} %param.13) | copy-start | bytes 442372
  118.6 50.4 %all-to-all-start = ((s32[1,256,32]{2,0,1:T(1,128)}), s32[1,256,32]{2,0,1:T(1,128)S(1)}, u32[]{:S(2)}, u32[]{:S(2)}) async-start(s32[1,256,32]{2,0,1:T(1,128)} %bitcast.5), calls=%async_computation | async-start | bytes 262144 | tf_op jit(solution)/shard_map/all_to_all | solution.py:102
  164.2 4.8 %copy-start.2 = (f32[4,256]{1,0:T(4,128)S(1)}, f32[4,256]{1,0:T(4,128)}, u32[]{:S(2)}) copy-start(f32[4,256]{1,0:T(4,128)} %param.15) | copy-start | bytes 12292
  169.7 24.6 %all-to-all-start.1 = ((bf16[128,4,256]{2,1,0:T(4,128)(2,1)}), bf16[128,4,256]{2,1,0:T(4,128)(2,1)S(1)}, u32[]{:S(2)}, u32[]{:S(2)}) async-start(bf16[128,4,256]{2,1,0:T(4,128)(2,1)} %stack.2), calls=%async_computation.1 | async-start | bytes 524288 | tf_op jit(solution)/shard_map/all_to_all | solution.py:66
  194.4 16.4 %all-to-all-start.2 = ((f32[128,1,576]{2,1,0:T(1,128)}), f32[128,1,576]{2,1,0:T(1,128)S(1)}, u32[]{:S(2)}, u32[]{:S(2)}) async-start(f32[128,1,576]{2,1,0:T(1,128)} %reshape.217), calls=%async_computation.2 | async-start | bytes 655360 | tf_op jit(solution)/shard_map/all_to_all | solution.py:95
  222.4 19.2 %all-to-all-start.3 = ((bf16[128,2,288]{2,1,0:T(2,128)(2,1)}), bf16[128,2,288]{2,1,0:T(2,128)(2,1)S(1)}, u32[]{:S(2)}, u32[]{:S(2)}) async-start(bf16[128,2,288]{2,1,0:T(2,128)(2,1)} %reshape.219), calls=%async_computation.3 | async-start | bytes 393216 | tf_op jit(solution)/shard_map/all_to_all | solution.py:117
  231.3 156.5 %all-reduce.3.cloned.1.call-start = ((), (), s32[]{:S(2)}) async-start(), calls=%async_computation.4 | async-start | bytes 1048576
Sparse Core Ops, SparseCore 0:
  241.0 146.7 all-reduce.2
